TPU v7x, 32 devices: a whole 2x2x4 slice. The times are simulated.
32 devices in a mesh: group: 2 (over y), slab: 4 (over z), subj: 2 (over x), yslab: 2 (over core).
Axes of the slice: x: 2, y: 2, z: 4, core: 2. Of those that a mesh axis runs over, the one named last changes fastest.
Arguments:
- subjects: bfloat16 [4, 64, 16, 256], P(('group', 'subj'), 'slab', 'yslab'), parts along dimension 0, may hold values from -6 to 6
- offsets: int32 [4, 3, 64, 16, 256], P(('group', 'subj'), None, 'slab', 'yslab'), parts along dimension 0, may hold values from -2 to 1
- template: float32 [128, 16, 256], P(('group', 'slab'), 'yslab'), parts along dimension 0, may hold values from -6 to 6
- control: float32 [4, 3, 19, 7, 128], P(('group', 'subj')), parts along dimension 0, may hold values from -8 to 8
Outputs:
- template_out: float32 [128, 16, 256], P(('group', 'slab'), 'yslab'), parts along dimension 0
- control_out: float32 [4, 3, 19, 7, 128], P(('group', 'subj')), parts along dimension 0
There are 2 independent parts, one for each index of `group`. A program takes and returns all parts, laid end to end along the dimension named above; each array names one. Nothing has to cross between parts.
All inputs are finite; a program needn't handle non-finite values.
Results may differ from a plain program's by a relative error of at most 0.00065.
Values may be sent and summed in bfloat16 or wider, within the bound.
A program may use at most 64 MiB of HBM per device.

v0:
```python
import jax
import jax.numpy as jnp
from jax import lax
from jax.sharding import PartitionSpec as P

KNOT = 4
KNOT_X = 2
HALO = 2
ITERS = 2
step_length = 0.5
tiny_term = 1e-06


def extended_2(value, sides, width):
    for axis, dim in sides:
        peers, length = (lax.axis_size(axis), value.shape[dim])
        up = [(i, (i + 1) % peers) for i in range(peers - 1)]
        down = [(j, i) for i, j in up]
        last = lax.slice_in_dim(value, length - width, length, axis=dim)
        initial = lax.slice_in_dim(value, 0, width, axis=dim)
        before = lax.ppermute(last, axis, up)
        after = lax.ppermute(initial, axis, down)
        value = jnp.concatenate([before, value, after], axis=dim)
    return value


def shifted(block, axis, distance):
    devices = range(lax.axis_size(axis))
    route = [(i - distance, i) for i in devices if i - distance in devices]
    return lax.ppermute(block, axis, route)


def from_root(value, axis, source):
    kept = jnp.where(lax.axis_index(axis) == source, value, 0).astype(value.dtype)
    return lax.psum(kept, axis)


def basis(positions, columns, spacing, wrap):
    cell = positions // spacing
    frac = (positions - cell * spacing).astype(jnp.float32) / spacing
    weights = [
        (1.0 - frac) ** 3 / 6.0,
        (3.0 * frac**3 - 6.0 * frac**2 + 4.0) / 6.0,
        (-3.0 * frac**3 + 3.0 * frac**2 + 3.0 * frac + 1.0) / 6.0,
        frac**3 / 6.0,
    ]
    index = jnp.arange(columns, dtype=jnp.int32)
    matrix = jnp.zeros((positions.shape[0], columns), jnp.float32)
    for offset in range(4):
        target = cell + offset
        if wrap:
            target = target % columns
        matrix = matrix + jnp.where(
            index[None, :] == target[:, None], weights[offset][:, None], 0.0
        )
    return matrix


def forward_field(coeffs, basis_z, basis_y, basis_x):
    high = lax.Precision.HIGHEST
    first = jnp.einsum("cabg,za->czbg", coeffs, basis_z, precision=high)
    second = jnp.einsum("czbg,yb->czyg", first, basis_y, precision=high)
    return jnp.einsum("czyg,xg->czyx", second, basis_x, precision=high)


def adjoint_field(gradient, basis_z, basis_y, basis_x):
    high = lax.Precision.HIGHEST
    first = jnp.einsum("czyx,xg->czyg", gradient, basis_x, precision=high)
    second = jnp.einsum("czyg,yb->czbg", first, basis_y, precision=high)
    return jnp.einsum("czbg,za->cabg", second, basis_z, precision=high)


def choose(shift_of, table, lead):
    result = table[-HALO + lead]
    for value in range(-HALO + 1, HALO):
        result = jnp.where(shift_of == value, table[value + lead], result)
    return result


def trilinear_local(volume, shifts, fraction, depth, height, width):
    frac_z, frac_y, frac_x = (fraction[0], fraction[1], fraction[2])
    shift_z, shift_y, shift_x = (shifts[0], shifts[1], shifts[2])
    along_y_of = {}
    diff_y_of = {}
    diff_xy_of = {}
    for move_z in range(-HALO, HALO + 1):
        along_x_of = {}
        diff_x_of = {}
        for move_y in range(-HALO, HALO + 1):
            plane = volume[
                move_z + HALO : move_z + HALO + depth, move_y + HALO : move_y + HALO + height, :
            ].astype(jnp.float32)
            columns = {}
            for move_x in range(-HALO, HALO + 1):
                columns[move_x] = plane[:, :, move_x + HALO : move_x + HALO + width]
            low = choose(shift_x, columns, 0)
            high = choose(shift_x, columns, 1)
            along_x_of[move_y] = low * (1.0 - frac_x) + high * frac_x
            diff_x_of[move_y] = high - low
        along_low = choose(shift_y, along_x_of, 0)
        along_high = choose(shift_y, along_x_of, 1)
        diff_low = choose(shift_y, diff_x_of, 0)
        diff_high = choose(shift_y, diff_x_of, 1)
        along_y_of[move_z] = along_low * (1.0 - frac_y) + along_high * frac_y
        diff_y_of[move_z] = along_high - along_low
        diff_xy_of[move_z] = diff_low * (1.0 - frac_y) + diff_high * frac_y
    along_y = [choose(shift_z, along_y_of, 0), choose(shift_z, along_y_of, 1)]
    diff_y = [choose(shift_z, diff_y_of, 0), choose(shift_z, diff_y_of, 1)]
    diff_xy = [choose(shift_z, diff_xy_of, 0), choose(shift_z, diff_xy_of, 1)]
    warped = along_y[0] * (1.0 - frac_z) + along_y[1] * frac_z
    slope_z = along_y[1] - along_y[0]
    slope_y = diff_y[0] * (1.0 - frac_z) + diff_y[1] * frac_z
    slope_x = diff_xy[0] * (1.0 - frac_z) + diff_xy[1] * frac_z
    return (warped, jnp.stack([slope_z, slope_y, slope_x]))


def shards(subjects, offsets, template, control):
    local_subjects = subjects.shape[0]
    depth, height, width = (subjects.shape[1], subjects.shape[2], subjects.shape[3])
    rows_slab = depth // KNOT
    cohort = local_subjects * lax.axis_size("subj")
    extended = extended_2(subjects, (("slab", 1), ("yslab", 2)), HALO)
    extended = jnp.pad(extended, ((0, 0), (0, 0), (0, 0), (HALO, HALO)))
    basis_z = basis(jnp.arange(depth, dtype=jnp.int32), rows_slab + 3, KNOT, False)
    y_start = lax.axis_index("yslab") * height
    basis_y = basis(y_start + jnp.arange(height, dtype=jnp.int32), control.shape[3], KNOT, False)
    basis_x = basis(jnp.arange(width, dtype=jnp.int32), control.shape[4], KNOT_X, True)
    first_row = lax.axis_index("slab") * rows_slab
    current = template
    coeffs_all = control
    for iteration in range(ITERS):
        band_coeffs = lax.dynamic_slice_in_dim(coeffs_all[0], first_row, rows_slab + 3, 1)
        displace = forward_field(band_coeffs, basis_z, basis_y, basis_x)
        tanh_u = jnp.tanh(displace)
        fraction = 0.5 + 0.5 * tanh_u
        warped, slopes = trilinear_local(extended[0], offsets[0], fraction, depth, height, width)
        resid = warped - current
        grad_u = resid[None] * slopes * (1.0 - tanh_u * tanh_u)
        band_list = [adjoint_field(grad_u, basis_z, basis_y, basis_x)]
        band_grid = jnp.stack(band_list)
        current = lax.psum(warped, "subj") / cohort
        band_grid = lax.psum(band_grid.astype(jnp.bfloat16), "yslab").astype(jnp.float32)
        head_rows = band_grid[:, :, :rows_slab]
        tail_part = band_grid[:, :, rows_slab:]
        carried = shifted(tail_part, "slab", 1)
        head_rows = head_rows.at[:, :, :3].add(carried)
        owned = lax.all_gather(head_rows.astype(jnp.bfloat16), "slab", axis=2, tiled=True).astype(
            head_rows.dtype
        )
        last_part = from_root(tail_part, "slab", lax.axis_size("slab") - 1)
        grid = jnp.concatenate([owned, last_part], axis=2)
        lengths = jnp.sqrt(jnp.sum(grid * grid, axis=1))
        peak = jnp.max(lengths, axis=(1, 2, 3))
        coeffs_all = coeffs_all - step_length * grid / (peak[:, None, None, None, None] + tiny_term)
    return (current, coeffs_all)


def solution(mesh):
    in_specs = (
        P(("group", "subj"), "slab", "yslab", None),
        P(("group", "subj"), None, "slab", "yslab", None),
        P(("group", "slab"), "yslab", None),
        P(("group", "subj"), None, None, None, None),
    )
    out_specs = (P(("group", "slab"), "yslab", None), P(("group", "subj"), None, None, None, None))
    return jax.shard_map(shards, mesh=mesh, in_specs=in_specs, out_specs=out_specs, check_vma=False)
```

profile of v0, /device:TPU:0, one launch (start us, length us, event | category | flops | bytes accessed | tf_op | source)
XLA Modules:
  0.0 160.3 jit_solution(13082636263804256856)
XLA Ops:
  7.2 0.7 fusion.363
  7.9 1.3 collective-permute-start.1
  9.2 5.6 %collective-permute-start = (bf16[1,2,8,256]{3,2,1,0:T(8,128)(2,1)S(1)}, bf16[1,2,8,256]{3,2,1,0:T(8,128)(2,1)S(1)}, u32[]{:S(2)}, u32[]{:S(2)}) collective-permute-start(bf16[1,2,8,256]{3,2,1,0:T(8,128)(2,1)S(1)} %get-tuple-element.162), channel_id=1, source_target_pairs={{0,4},{4,8},{8,12},{1,5},{5,9},{9,13},{2,6},{6,10},{10,14},{3,7},{... | collective-permute-start | bytes 24584 | tf_op jit(solution)/shard_map/ppermute | solution.py:21
  15.2 0.9 constant_dynamic-slice_fusion
  16.2 0.4 convolution_bitcast_fusion.3
  16.7 0.4 convolution_bitcast_fusion.1
  17.1 0.4 copy-done.65
  17.6 1.5 collective-permute-start.2
  19.0 1.3 collective-permute-start.3
  20.4 1.5 multiply_add_fusion.1
  21.9 0.2 collective-permute-done.3
  22.1 0.3 fusion.26
  22.5 0.3 slice_convert_fusion.8
  22.8 0.6 copy-done.59
  23.5 0.2 fusion.52
  23.7 0.3 fusion.38
  24.0 0.2 fusion.40
  24.2 0.3 fusion.46
  24.6 0.3 fusion.44
  24.9 0.6 copy-done.64
  25.5 3.3 %fusion.335 = (f32[16,8,256]{2,1,0:T(8,128)S(1)}, f32[16,8,256]{2,1,0:T(8,128)}, f32[16,8,256]{2,1,0:T(8,128)S(1)}, f32[16,8,256]{2,1,0:T(8,128)S(1)}, f32[16,8,...) fusion(f32[16,8,256]{2,1,0:T(8,128)S(1)} %copy-done.64, ...), kind=kLoop, calls=%fused_computation.598 | loop fusion | flops 8093696 | bytes 21266432 | tf_op jit(solution)/shard_map/sub | solution.py:137
  29.0 0.1 add_bitcast_fusion.3
  29.1 0.3 copy-done.1
  30.5 2.9 %add_bitcast_fusion.2 = (f32[1,16,8,256]{3,2,1,0:T(8,128)S(1)}, f32[16,8,256]{2,1,0:T(8,128)}, f32[16,8,256]{2,1,0:T(8,128)}, f32[16,8,256]{2,1,0:T(8,128)}, f32...) fusion(pred[1,1,16,8,256]{4,3,2,1,0:T(8,128)(4,1)S(1)} %get-tup, ...), kind=kLoop, calls=%fused_computation.248 | loop fusion | flops 2654208 | bytes 8454144 | tf_op jit(solution)/shard_map/stack | solution.py:114
  33.4 0.6 copy-done.70
  34.1 0.8 fusion.4
  35.1 0.4 fusion.217
  35.6 0.1 copy-done.98
  35.7 0.2 fusion
  35.9 4.2 %psum.42 = bf16[1,3,7,7,128]{4,2,3,1,0:T(8,128)(2,1)S(1)} all-reduce(bf16[1,3,7,7,128]{4,2,3,1,0:T(8,128)(2,1)S(1)} %fusion), channel_id=1, replica_groups=mesh['group'=2,'slab'=4,'subj'=2,'yslab'=2] {'yslab'}, use_global_device_ids=true, to_apply=%region_0.1 | all-reduce | flops 18816 | bytes 75264 | tf_op jit(solution)/shard_map/psum | solution.py:142
  40.2 0.6 copy-done.45
  40.8 3.8 %collective-permute-start.4 = (f32[1,3,3,7,128]{4,2,3,1,0:T(4,128)S(1)}, f32[1,3,3,7,128]{4,2,3,1,0:T(4,128)S(1)}, u32[]{:S(2)}, u32[]{:S(2)}) collective-permute-start(f32[1,3,3,7,128]{4,2,3,1,0:T(4,128)S(1)} %slice.1053), channel_id=1, source_target_pairs={{0,4},{4,8},{8,12},{1,5},{5,9},{9,13},{2,6},{6,10},{10,14},{3,7},{... | collective-permute-start | bytes 96776 | tf_op jit(solution)/shard_map/ppermute | solution.py:30
  44.6 17.6 %psum.43 = f32[1,3,3,7,128]{4,2,3,1,0:T(4,128)S(1)} all-reduce(f32[1,3,3,7,128]{4,2,3,1,0:T(4,128)S(1)} %broadcast_select_fusion.1), channel_id=1, replica_groups=mesh['group'=2,'slab'=4,'subj'=2,'yslab'=2] {'slab'}, use_global_device_ids=true, to_apply=%region_1.2 | all-reduce | flops 8064 | bytes 64512 | tf_op jit(solution)/shard_map/psum | solution.py:35
  62.3 0.7 slice-done
  63.0 0.1 scatter-add.6
  63.2 13.4 %all_gather.6 = bf16[1,3,16,7,128]{4,3,1,0,2:T(8,128)(2,1)S(1)} all-gather(bf16[1,3,4,7,128]{4,3,1,0,2:T(8,128)(2,1)S(1)} %copy.8), channel_id=1, replica_groups=mesh['group'=2,'slab'=4,'subj'=2,'yslab'=2] {'slab'}, dimensions={2}, use_global_device_ids=true | all-gather | bytes 107520 | tf_op jit(solution)/shard_map/all_gather | solution.py:147
  76.6 0.7 fusion.174
  78.1 1.1 copy_subtract_fusion
  79.2 0.4 convolution_bitcast_fusion.2
  79.7 0.4 convolution_bitcast_fusion
  80.2 1.5 multiply_add_fusion
  81.9 3.0 %subtract_bitcast_fusion = (f32[1,16,8,256]{3,2,1,0:T(8,128)}, f32[16,8,256]{2,1,0:T(8,128)S(1)}, f32[16,8,256]{2,1,0:T(8,128)S(1)}, f32[16,8,256]{2,1,0:T(8,128...) fusion(pred[1,1,16,8,256]{4,3,2,1,0:T(8,128)(4,1)S(1)} %get-tup, ...), kind=kLoop, calls=%fused_computation.191 | loop fusion | flops 4227072 | bytes 8716288 | tf_op jit(solution)/shard_map/stack | solution.py:114
  84.9 0.8 add_bitcast_fusion.1
  85.9 0.1 copy-done.52
  86.2 0.5 copy-done.47
  86.8 0.2 add_bitcast_fusion
  87.0 20.5 %all-reduce.4.cloned.1.call-done = (f32[16,8,256]{2,1,0:T(8,128)}, f32[16,8,256]{2,1,0:T(8,128)}) async-done(((f32[16,8,256]{2,1,0:T(8,128)}, f32[16,8,256]{2,1,0:T(8,128)}), (f32[16,8,256]{2,1,0:T(8,128)}, f32[16,8,256]{2,1,0:T(8,128)})) %all-reduce.4.cloned.1.call-update) | async-done | bytes 262160 | tf_op jit(solution)/shard_map/psum | solution.py:141
  107.5 0.9 multiply_subtract_fusion
  108.5 0.6 copy-done.68
  109.1 0.8 fusion.11
  110.1 0.4 fusion.214
  110.6 0.1 copy-done.99
  110.7 0.2 fusion.1
  111.0 3.5 %psum.46 = bf16[1,3,7,7,128]{4,2,3,1,0:T(8,128)(2,1)S(1)} all-reduce(bf16[1,3,7,7,128]{4,2,3,1,0:T(8,128)(2,1)S(1)} %fusion.1), channel_id=1, replica_groups=mesh['group'=2,'slab'=4,'subj'=2,'yslab'=2] {'yslab'}, use_global_device_ids=true, to_apply=%region_6.7 | all-reduce | flops 18816 | bytes 75264 | tf_op jit(solution)/shard_map/psum | solution.py:142
  114.5 0.6 copy-done.46
  115.1 0.3 copy-done.63
  115.4 0.7 broadcast_multiply_fusion
  116.1 3.4 %collective-permute-start.5 = (f32[1,3,3,7,128]{4,2,3,1,0:T(4,128)S(1)}, f32[1,3,3,7,128]{4,2,3,1,0:T(4,128)S(1)}, u32[]{:S(2)}, u32[]{:S(2)}) collective-permute-start(f32[1,3,3,7,128]{4,2,3,1,0:T(4,128)S(1)} %slice.1059), channel_id=1, source_target_pairs={{0,4},{4,8},{8,12},{1,5},{5,9},{9,13},{2,6},{6,10},{10,14},{3,7},{... | collective-permute-start | bytes 96776 | tf_op jit(solution)/shard_map/ppermute | solution.py:30
  119.5 17.6 %psum.47 = f32[1,3,3,7,128]{4,2,3,1,0:T(4,128)S(1)} all-reduce(f32[1,3,3,7,128]{4,2,3,1,0:T(4,128)S(1)} %broadcast_select_fusion), channel_id=1, replica_groups=mesh['group'=2,'slab'=4,'subj'=2,'yslab'=2] {'slab'}, use_global_device_ids=true, to_apply=%region_7.8 | all-reduce | flops 8064 | bytes 64512 | tf_op jit(solution)/shard_map/psum | solution.py:35
  137.1 0.7 slice-done.1
  137.8 0.1 scatter-add.9
  138.0 13.2 %all_gather.7 = bf16[1,3,16,7,128]{4,3,1,0,2:T(8,128)(2,1)S(1)} all-gather(bf16[1,3,4,7,128]{4,3,1,0,2:T(8,128)(2,1)S(1)} %copy.12), channel_id=1, replica_groups=mesh['group'=2,'slab'=4,'subj'=2,'yslab'=2] {'slab'}, dimensions={2}, use_global_device_ids=true | all-gather | bytes 107520 | tf_op jit(solution)/shard_map/all_gather | solution.py:147
  151.3 0.6 fusion.173
  152.6 0.9 copy.15
  (312 shorter events, 2.8 us)
Async XLA Ops:
  7.2 100.3 %all-reduce.4.cloned.1.call-start = ((), (), s32[]{:S(2)}) async-start(), calls=%async_computation | async-start | bytes 524288 | tf_op jit(solution)/shard_map/psum | solution.py:141
  7.9 9.6 %collective-permute-start.1 = (bf16[1,2,8,256]{3,2,1,0:T(8,128)(2,1)S(1)}, bf16[1,2,8,256]{3,2,1,0:T(8,128)(2,1)S(1)}, u32[]{:S(2)}, u32[]{:S(2)}) collective-permute-start(bf16[1,2,8,256]{3,2,1,0:T(8,128)(2,1)S(1)} %get-tuple-element.161), channel_id=1, source_target_pairs={{4,0},{8,4},{12,8},{5,1},{9,5},{13,9},{6,2},{10,6},{14,10},{7,3},{... | collective-permute-start | bytes 24584 | tf_op jit(solution)/shard_map/ppermute | solution.py:22
  9.2 7.9 %collective-permute-start = (bf16[1,2,8,256]{3,2,1,0:T(8,128)(2,1)S(1)}, bf16[1,2,8,256]{3,2,1,0:T(8,128)(2,1)S(1)}, u32[]{:S(2)}, u32[]{:S(2)}) collective-permute-start(bf16[1,2,8,256]{3,2,1,0:T(8,128)(2,1)S(1)} %get-tuple-element.162), channel_id=1, source_target_pairs={{0,4},{4,8},{8,12},{1,5},{5,9},{9,13},{2,6},{6,10},{10,14},{3,7},{... | collective-permute-start | bytes 24584 | tf_op jit(solution)/shard_map/ppermute | solution.py:21
  14.8 1.7 %copy-start.109 = (f32[8]{0:T(128)}, f32[8]{0:T(128)S(1)}, u32[]{:S(2)}) copy-start(f32[8]{0:T(128)S(1)} %get-tuple-element.178) | copy-start | bytes 100
  14.8 1.7 %copy-start.112 = (f32[8]{0:T(128)}, f32[8]{0:T(128)S(1)}, u32[]{:S(2)}) copy-start(f32[8]{0:T(128)S(1)} %get-tuple-element.179) | copy-start | bytes 100
  14.9 1.7 %copy-start.116 = (s32[8]{0:T(128)}, s32[8]{0:T(128)S(1)}, u32[]{:S(2)}) copy-start(s32[8]{0:T(128)S(1)} %get-tuple-element.182) | copy-start | bytes 100
  14.9 1.7 %copy-start.120 = (s32[8]{0:T(128)}, s32[8]{0:T(128)S(1)}, u32[]{:S(2)}) copy-start(s32[8]{0:T(128)S(1)} %get-tuple-element.183) | copy-start | bytes 100
  14.9 1.7 %copy-start.124 = (s32[8]{0:T(128)}, s32[8]{0:T(128)S(1)}, u32[]{:S(2)}) copy-start(s32[8]{0:T(128)S(1)} %get-tuple-element.170) | copy-start | bytes 100
  14.9 1.7 %copy-start.128 = (s32[8]{0:T(128)}, s32[8]{0:T(128)S(1)}, u32[]{:S(2)}) copy-start(s32[8]{0:T(128)S(1)} %get-tuple-element.171) | copy-start | bytes 100
  15.0 1.7 %copy-start.132 = (f32[8]{0:T(128)}, f32[8]{0:T(128)S(1)}, u32[]{:S(2)}) copy-start(f32[8]{0:T(128)S(1)} %get-tuple-element.172) | copy-start | bytes 100
  15.0 1.7 %copy-start.136 = (f32[8]{0:T(128)}, f32[8]{0:T(128)S(1)}, u32[]{:S(2)}) copy-start(f32[8]{0:T(128)S(1)} %get-tuple-element.173) | copy-start | bytes 100
  15.1 18.2 %copy-start.66 = (f32[256]{0:T(256)}, f32[256]{0:T(256)S(1)}, u32[]{:S(2)}) copy-start(f32[256]{0:T(256)S(1)} %get-tuple-element.189) | copy-start | bytes 3076
  15.2 5.2 %copy-start.69 = (s32[256]{0:T(256)}, s32[256]{0:T(256)S(1)}, u32[]{:S(2)}) copy-start(s32[256]{0:T(256)S(1)} %get-tuple-element.186) | copy-start | bytes 3076
  15.2 5.2 %copy-start.73 = (s32[256]{0:T(256)}, s32[256]{0:T(256)S(1)}, u32[]{:S(2)}) copy-start(s32[256]{0:T(256)S(1)} %get-tuple-element.187) | copy-start | bytes 3076
  17.1 3.3 %copy-start.77 = (s32[256]{0:T(256)}, s32[256]{0:T(256)S(1)}, u32[]{:S(2)}) copy-start(s32[256]{0:T(256)S(1)} %get-tuple-element.184) | copy-start | bytes 3076
  17.1 3.3 %copy-start.81 = (s32[256]{0:T(256)}, s32[256]{0:T(256)S(1)}, u32[]{:S(2)}) copy-start(s32[256]{0:T(256)S(1)} %get-tuple-element.185) | copy-start | bytes 3076
  17.6 4.3 %collective-permute-start.2 = (bf16[1,20,2,256]{3,2,1,0:T(2,128)(2,1)S(1)}, bf16[1,20,2,256]{3,2,1,0:T(2,128)(2,1)S(1)}, u32[]{:S(2)}, u32[]{:S(2)}) collective-permute-start(bf16[1,20,2,256]{3,2,1,0:T(2,128)(2,1)S(1)} %get-tuple-element.159), channel_id=1, source_target_pairs={{0,1},{2,3},{4,5},{6,7},{8,9},{10,11},{12,13},{14,15},{16,17},{18,... | collective-permute-start | bytes 61448 | tf_op jit(solution)/shard_map/ppermute | solution.py:21
  19.0 3.1 %collective-permute-start.3 = (bf16[1,20,2,256]{3,2,1,0:T(2,128)(2,1)S(1)}, bf16[1,20,2,256]{3,2,1,0:T(2,128)(2,1)S(1)}, u32[]{:S(2)}, u32[]{:S(2)}) collective-permute-start(bf16[1,20,2,256]{3,2,1,0:T(2,128)(2,1)S(1)} %get-tuple-element.160), channel_id=1, source_target_pairs={{1,0},{3,2},{5,4},{7,6},{9,8},{11,10},{13,12},{15,14},{17,16},{19,... | collective-permute-start | bytes 61448 | tf_op jit(solution)/shard_map/ppermute | solution.py:22
  29.0 1.5 copy-start.44
  29.0 1.5 copy-start.60
  30.5 2.9 %copy-start.57 = (f32[3,16,8,256]{3,2,1,0:T(8,128)S(1)}, f32[3,16,8,256]{3,2,1,0:T(8,128)}, u32[]{:S(2)}) copy-start(f32[3,16,8,256]{3,2,1,0:T(8,128)} %get-tuple-element.164) | copy-start | bytes 1179652
  30.5 2.9 %copy-start.74 = (s32[256]{0:T(256)S(1)}, s32[256]{0:T(256)}, u32[]{:S(2)}) copy-start(s32[256]{0:T(256)} %copy-done.73) | copy-start | bytes 3076
  30.5 2.9 %copy-start.78 = (s32[256]{0:T(256)S(1)}, s32[256]{0:T(256)}, u32[]{:S(2)}) copy-start(s32[256]{0:T(256)} %copy-done.77) | copy-start | bytes 3076
  30.5 2.9 %copy-start.82 = (s32[256]{0:T(256)S(1)}, s32[256]{0:T(256)}, u32[]{:S(2)}) copy-start(s32[256]{0:T(256)} %copy-done.81) | copy-start | bytes 3076
  40.8 21.4 %collective-permute-start.4 = (f32[1,3,3,7,128]{4,2,3,1,0:T(4,128)S(1)}, f32[1,3,3,7,128]{4,2,3,1,0:T(4,128)S(1)}, u32[]{:S(2)}, u32[]{:S(2)}) collective-permute-start(f32[1,3,3,7,128]{4,2,3,1,0:T(4,128)S(1)} %slice.1053), channel_id=1, source_target_pairs={{0,4},{4,8},{8,12},{1,5},{5,9},{9,13},{2,6},{6,10},{10,14},{3,7},{... | collective-permute-start | bytes 96776 | tf_op jit(solution)/shard_map/ppermute | solution.py:30
  77.9 1.7 %copy-start.114 = (f32[8]{0:T(128)S(1)}, f32[8]{0:T(128)}, u32[]{:S(2)}) copy-start(f32[8]{0:T(128)} %copy-done.112) | copy-start | bytes 100
  77.9 1.7 %copy-start.118 = (s32[8]{0:T(128)S(1)}, s32[8]{0:T(128)}, u32[]{:S(2)}) copy-start(s32[8]{0:T(128)} %copy-done.116) | copy-start | bytes 100
  77.9 1.7 %copy-start.122 = (s32[8]{0:T(128)S(1)}, s32[8]{0:T(128)}, u32[]{:S(2)}) copy-start(s32[8]{0:T(128)} %copy-done.120) | copy-start | bytes 100
  78.0 1.7 %copy-start.126 = (s32[8]{0:T(128)S(1)}, s32[8]{0:T(128)}, u32[]{:S(2)}) copy-start(s32[8]{0:T(128)} %copy-done.124) | copy-start | bytes 100
  78.0 1.7 %copy-start.130 = (s32[8]{0:T(128)S(1)}, s32[8]{0:T(128)}, u32[]{:S(2)}) copy-start(s32[8]{0:T(128)} %copy-done.128) | copy-start | bytes 100
  78.0 1.7 %copy-start.134 = (f32[8]{0:T(128)S(1)}, f32[8]{0:T(128)}, u32[]{:S(2)}) copy-start(f32[8]{0:T(128)} %copy-done.132) | copy-start | bytes 100
  78.0 1.7 %copy-start.138 = (f32[8]{0:T(128)S(1)}, f32[8]{0:T(128)}, u32[]{:S(2)}) copy-start(f32[8]{0:T(128)} %copy-done.136) | copy-start | bytes 100
  78.0 2.1 %copy-start.71 = (s32[256]{0:T(256)S(1)}, s32[256]{0:T(256)}, u32[]{:S(2)}) copy-start(s32[256]{0:T(256)} %copy-done.69) | copy-start | bytes 3076
  78.0 2.1 %copy-start.75 = (s32[256]{0:T(256)S(1)}, s32[256]{0:T(256)}, u32[]{:S(2)}) copy-start(s32[256]{0:T(256)} %copy-done.73) | copy-start | bytes 3076
  78.0 2.1 %copy-start.79 = (s32[256]{0:T(256)S(1)}, s32[256]{0:T(256)}, u32[]{:S(2)}) copy-start(s32[256]{0:T(256)} %copy-done.77) | copy-start | bytes 3076
  78.0 2.1 %copy-start.83 = (s32[256]{0:T(256)S(1)}, s32[256]{0:T(256)}, u32[]{:S(2)}) copy-start(s32[256]{0:T(256)} %copy-done.81) | copy-start | bytes 3076
  78.0 3.7 %copy-start.30 = (f32[16,8,256]{2,1,0:T(8,128)S(1)}, f32[16,8,256]{2,1,0:T(8,128)}, u32[]{:S(2)}) copy-start(f32[16,8,256]{2,1,0:T(8,128)} %copy-done.29) | copy-start | bytes 393220
  78.0 3.7 %copy-start.32 = (f32[16,8,256]{2,1,0:T(8,128)S(1)}, f32[16,8,256]{2,1,0:T(8,128)}, u32[]{:S(2)}) copy-start(f32[16,8,256]{2,1,0:T(8,128)} %copy-done.31) | copy-start | bytes 393220
  78.1 3.7 %copy-start.34 = (f32[16,8,256]{2,1,0:T(8,128)S(1)}, f32[16,8,256]{2,1,0:T(8,128)}, u32[]{:S(2)}) copy-start(f32[16,8,256]{2,1,0:T(8,128)} %copy-done.33) | copy-start | bytes 393220
  78.1 3.7 %copy-start.36 = (f32[16,8,256]{2,1,0:T(8,128)S(1)}, f32[16,8,256]{2,1,0:T(8,128)}, u32[]{:S(2)}) copy-start(f32[16,8,256]{2,1,0:T(8,128)} %copy-done.35) | copy-start | bytes 393220
  78.1 3.7 %copy-start.38 = (f32[16,8,256]{2,1,0:T(8,128)S(1)}, f32[16,8,256]{2,1,0:T(8,128)}, u32[]{:S(2)}) copy-start(f32[16,8,256]{2,1,0:T(8,128)} %copy-done.37) | copy-start | bytes 393220
  79.1 2.6 %copy-start.28 = (f32[16,8,256]{2,1,0:T(8,128)S(1)}, f32[16,8,256]{2,1,0:T(8,128)}, u32[]{:S(2)}) copy-start(f32[16,8,256]{2,1,0:T(8,128)} %copy-done.27) | copy-start | bytes 393220
  79.2 2.6 %copy-start.24 = (f32[16,8,256]{2,1,0:T(8,128)S(1)}, f32[16,8,256]{2,1,0:T(8,128)}, u32[]{:S(2)}) copy-start(f32[16,8,256]{2,1,0:T(8,128)} %copy-done.23) | copy-start | bytes 393220
  79.2 2.6 %copy-start.26 = (f32[16,8,256]{2,1,0:T(8,128)S(1)}, f32[16,8,256]{2,1,0:T(8,128)}, u32[]{:S(2)}) copy-start(f32[16,8,256]{2,1,0:T(8,128)} %copy-done.25) | copy-start | bytes 393220
  79.7 2.2 %copy-start.16 = (f32[16,8,256]{2,1,0:T(8,128)S(1)}, f32[16,8,256]{2,1,0:T(8,128)}, u32[]{:S(2)}) copy-start(f32[16,8,256]{2,1,0:T(8,128)} %copy-done.15) | copy-start | bytes 393220
  79.7 2.2 %copy-start.18 = (f32[16,8,256]{2,1,0:T(8,128)S(1)}, f32[16,8,256]{2,1,0:T(8,128)}, u32[]{:S(2)}) copy-start(f32[16,8,256]{2,1,0:T(8,128)} %copy-done.17) | copy-start | bytes 393220
  79.7 2.2 %copy-start.20 = (f32[16,8,256]{2,1,0:T(8,128)S(1)}, f32[16,8,256]{2,1,0:T(8,128)}, u32[]{:S(2)}) copy-start(f32[16,8,256]{2,1,0:T(8,128)} %copy-done.19) | copy-start | bytes 393220
  79.7 2.2 %copy-start.22 = (f32[16,8,256]{2,1,0:T(8,128)S(1)}, f32[16,8,256]{2,1,0:T(8,128)}, u32[]{:S(2)}) copy-start(f32[16,8,256]{2,1,0:T(8,128)} %copy-done.21) | copy-start | bytes 393220
  80.1 1.7 %copy-start.2 = (f32[16,8,256]{2,1,0:T(8,128)S(1)}, f32[16,8,256]{2,1,0:T(8,128)}, u32[]{:S(2)}) copy-start(f32[16,8,256]{2,1,0:T(8,128)} %copy-done.1) | copy-start | bytes 393220
  80.2 1.7 %copy-start.4 = (f32[16,8,256]{2,1,0:T(8,128)S(1)}, f32[16,8,256]{2,1,0:T(8,128)}, u32[]{:S(2)}) copy-start(f32[16,8,256]{2,1,0:T(8,128)} %copy-done.3) | copy-start | bytes 393220
  80.2 1.7 %copy-start.6 = (f32[16,8,256]{2,1,0:T(8,128)S(1)}, f32[16,8,256]{2,1,0:T(8,128)}, u32[]{:S(2)}) copy-start(f32[16,8,256]{2,1,0:T(8,128)} %copy-done.5) | copy-start | bytes 393220
  80.2 1.7 %copy-start.8 = (f32[16,8,256]{2,1,0:T(8,128)S(1)}, f32[16,8,256]{2,1,0:T(8,128)}, u32[]{:S(2)}) copy-start(f32[16,8,256]{2,1,0:T(8,128)} %copy-done.7) | copy-start | bytes 393220
  80.2 1.7 %copy-start.10 = (f32[16,8,256]{2,1,0:T(8,128)S(1)}, f32[16,8,256]{2,1,0:T(8,128)}, u32[]{:S(2)}) copy-start(f32[16,8,256]{2,1,0:T(8,128)} %copy-done.9) | copy-start | bytes 393220
  80.2 1.7 %copy-start.12 = (f32[16,8,256]{2,1,0:T(8,128)S(1)}, f32[16,8,256]{2,1,0:T(8,128)}, u32[]{:S(2)}) copy-start(f32[16,8,256]{2,1,0:T(8,128)} %copy-done.11) | copy-start | bytes 393220
  80.2 1.7 %copy-start.14 = (f32[16,8,256]{2,1,0:T(8,128)S(1)}, f32[16,8,256]{2,1,0:T(8,128)}, u32[]{:S(2)}) copy-start(f32[16,8,256]{2,1,0:T(8,128)} %copy-done.13) | copy-start | bytes 393220
  80.2 1.7 %copy-start.61 = (pred[1,1,16,8,256]{4,3,2,1,0:T(8,128)(4,1)S(1)}, pred[1,1,16,8,256]{4,3,2,1,0:T(8,128)(4,1)}, u32[]{:S(2)}) copy-start(pred[1,1,16,8,256]{4,3,2,1,0:T(8,128)(4,1)} %copy-done.60) | copy-start | bytes 98308
  86.8 20.7 %copy-start = (f32[16,8,256]{2,1,0:T(8,128)S(1)}, f32[16,8,256]{2,1,0:T(8,128)}, u32[]{:S(2)}) copy-start(f32[16,8,256]{2,1,0:T(8,128)} %get-tuple-element.116) | copy-start | bytes 393220
  86.8 21.6 %copy-start.62 = (f32[1,16,8,256]{3,2,1,0:T(8,128)S(1)}, f32[1,16,8,256]{3,2,1,0:T(8,128)}, u32[]{:S(2)}) copy-start(f32[1,16,8,256]{3,2,1,0:T(8,128)} %get-tuple-element.32) | copy-start | bytes 393220
  86.8 21.6 %copy-start.72 = (s32[256]{0:T(256)S(1)}, s32[256]{0:T(256)}, u32[]{:S(2)}) copy-start(s32[256]{0:T(256)} %copy-done.69) | copy-start | bytes 3076
  86.8 21.7 %copy-start.76 = (s32[256]{0:T(256)S(1)}, s32[256]{0:T(256)}, u32[]{:S(2)}) copy-start(s32[256]{0:T(256)} %copy-done.73) | copy-start | bytes 3076
  86.8 21.7 %copy-start.80 = (s32[256]{0:T(256)S(1)}, s32[256]{0:T(256)}, u32[]{:S(2)}) copy-start(s32[256]{0:T(256)} %copy-done.77) | copy-start | bytes 3076
  86.8 21.7 %copy-start.84 = (s32[256]{0:T(256)S(1)}, s32[256]{0:T(256)}, u32[]{:S(2)}) copy-start(s32[256]{0:T(256)} %copy-done.81) | copy-start | bytes 3076
  87.0 21.5 %copy-start.58 = (f32[3,16,8,256]{3,2,1,0:T(8,128)S(1)}, f32[3,16,8,256]{3,2,1,0:T(8,128)}, u32[]{:S(2)}) copy-start(f32[3,16,8,256]{3,2,1,0:T(8,128)} %get-tuple-element.167) | copy-start | bytes 1179652
  116.1 21.0 %collective-permute-start.5 = (f32[1,3,3,7,128]{4,2,3,1,0:T(4,128)S(1)}, f32[1,3,3,7,128]{4,2,3,1,0:T(4,128)S(1)}, u32[]{:S(2)}, u32[]{:S(2)}) collective-permute-start(f32[1,3,3,7,128]{4,2,3,1,0:T(4,128)S(1)} %slice.1059), channel_id=1, source_target_pairs={{0,4},{4,8},{8,12},{1,5},{5,9},{9,13},{2,6},{6,10},{10,14},{3,7},{... | collective-permute-start | bytes 96776 | tf_op jit(solution)/shard_map/ppermute | solution.py:30
  (85 other events, 78.3 us)
Sparse Core Ops, SparseCore 0:
  85.9 21.5 all-reduce.3
where the time goes:
time: 161 us; the launch traced here: 160 us
  blocking collectives  69.6 us (43%)
  waiting for transfers between devices  20.7 us (13%)
  between operations  17.3 us (11%)
  starting transfers between devices  16.8 us (10%)
  other arithmetic  16.6 us (10%)
  local copies, waits for them, and re-layouts  11.8 us (7%)
  matrix products  7.5 us (5%)
    psum x2, blocking collectives, from_root(): return lax.psum(kept, axis)  35.2 us
    all_gather x2, blocking collectives, shards(): lax.all_gather(head_rows.astype(jnp.bfloat16), 'slab', axis=2, tiled=True)  26.7 us
    psum x1, waiting for transfers between devices, shards(): current = lax.psum(warped, 'subj') / cohort  20.5 us
    unnamed x283, local copies, waits for them, and re-layouts  8.37 us
    psum x2, blocking collectives, shards(): lax.psum(band_grid.astype(jnp.bfloat16), 'yslab').astype(jnp.float32)  7.77 us
    ppermute x2, starting transfers between devices, shifted(): return lax.ppermute(block, axis, route)  7.15 us
    ppermute x2, starting transfers between devices, extended_2(): before = lax.ppermute(last, axis, up)  7.04 us
    another operation x6, other arithmetic, trilinear_local(): return (warped, jnp.stack([slope_z, slope_y, slope_x]))  6.89 us
  transfers between devices with their start and end apart: 7, of which 2 were waited for; matrix products, arithmetic and copies ran while one was open for 2% of the time, Pallas kernels for 0%

commit v1 on v0

--- a/solution.py
+++ b/solution.py
@@ -32,7 +32,7 @@
 
 def from_root(value, axis, source):
     kept = jnp.where(lax.axis_index(axis) == source, value, 0).astype(value.dtype)
-    return lax.psum(kept, axis)
+    return jnp.sum(lax.all_gather(kept, axis), 0)
 
 
 def basis(positions, columns, spacing, wrap):

time: 161 us -> 155 us (0.963)
  blocking collectives: 69.6 us -> 61.4 us
    psum x2 -> x0, blocking collectives: 35.2 us -> none  [from_root(): return lax.psum(kept, axis)]
    all_gather x0 -> x2, blocking collectives: none -> 26.9 us  [from_root(): return jnp.sum(lax.all_gather(kept, axis), 0)]
    unnamed x283 -> x289, local copies, waits for them, and re-layouts: 8.37 us -> 8.64 us
where the time goes in v1:
time: 155 us; the launch traced here: 154 us
  blocking collectives  61.4 us (40%)
  waiting for transfers between devices  21.8 us (14%)
  between operations  17.4 us (11%)
  starting transfers between devices  16.8 us (11%)
  other arithmetic  16.7 us (11%)
  local copies, waits for them, and re-layouts  12.1 us (8%)
  matrix products  7.96 us (5%)
    all_gather x2, blocking collectives, from_root(): return jnp.sum(lax.all_gather(kept, axis), 0)  26.9 us
    all_gather x2, blocking collectives, shards(): lax.all_gather(head_rows.astype(jnp.bfloat16), 'slab', axis=2, tiled=True)  26.8 us
    psum x1, waiting for transfers between devices, shards(): current = lax.psum(warped, 'subj') / cohort  21.6 us
    unnamed x289, local copies, waits for them, and re-layouts  8.64 us
    psum x2, blocking collectives, shards(): lax.psum(band_grid.astype(jnp.bfloat16), 'yslab').astype(jnp.float32)  7.77 us
    ppermute x2, starting transfers between devices, shifted(): return lax.ppermute(block, axis, route)  7.15 us
    ppermute x2, starting transfers between devices, extended_2(): before = lax.ppermute(last, axis, up)  7.04 us
    another operation x6, other arithmetic, trilinear_local(): return (warped, jnp.stack([slope_z, slope_y, slope_x]))  6.94 us
  transfers between devices with their start and end apart: 7, of which 2 were waited for; matrix products, arithmetic and copies ran while one was open for 2% of the time, Pallas kernels for 0%

profile of v1, /device:TPU:0, one launch (start us, length us, event | category | flops | bytes accessed | tf_op | source)
XLA Modules:
  0.0 154.2 jit_solution(13176367162725013996)
XLA Ops:
  7.2 0.7 fusion.360
  7.9 1.3 collective-permute-start.1
  9.2 5.6 %collective-permute-start = (bf16[1,2,8,256]{3,2,1,0:T(8,128)(2,1)S(1)}, bf16[1,2,8,256]{3,2,1,0:T(8,128)(2,1)S(1)}, u32[]{:S(2)}, u32[]{:S(2)}) collective-permute-start(bf16[1,2,8,256]{3,2,1,0:T(8,128)(2,1)S(1)} %get-tuple-element.164), channel_id=1, source_target_pairs={{0,4},{4,8},{8,12},{1,5},{5,9},{9,13},{2,6},{6,10},{10,14},{3,7},{... | collective-permute-start | bytes 24584 | tf_op jit(solution)/shard_map/ppermute | solution.py:21
  15.2 0.9 constant_dynamic-slice_fusion.1
  16.2 0.4 convolution_bitcast_fusion.5
  16.7 0.4 convolution_bitcast_fusion.3
  17.1 0.4 copy-done.64
  17.6 1.5 collective-permute-start.2
  19.0 1.3 collective-permute-start.3
  20.4 1.5 %multiply_add_fusion.1 = (f32[3,16,8,256]{3,2,1,0:T(8,128)S(1)}, f32[3,16,8,256]{3,2,1,0:T(8,128)}) fusion(f32[3,16,8,128]{3,2,1,0:T(8,128)S(1)} %convolution_bitcast_fusion.3, f32[256]{0:T(256)S(1)} %get-tuple-element.193, s32[256]{0:T(256)S(1)} %get-tuple-element.186, f32[256]{0:T(256)S(1)} %get-tuple-element.192, s32[256]{0:T(256)S(1)} %get-tuple-element.187, ...), kind=kOutput, calls=%fused_computation.34 | convolution fusion | flops 151552000 | bytes 991232 | tf_op jit(solution)/shard_map/czyg,xg->czyx/dot_general | solution.py:63
  21.9 0.2 collective-permute-done.3
  22.1 0.3 fusion.26
  22.5 0.3 slice_convert_fusion.8
  22.8 0.6 copy-done.59
  23.5 0.2 fusion.50
  23.7 0.3 fusion.36
  24.0 0.2 fusion.38
  24.2 0.3 fusion.44
  24.6 0.3 fusion.42
  24.9 0.6 copy-done.63
  25.5 3.3 %fusion.332 = (f32[16,8,256]{2,1,0:T(8,128)S(1)}, f32[16,8,256]{2,1,0:T(8,128)}, f32[16,8,256]{2,1,0:T(8,128)S(1)}, f32[16,8,256]{2,1,0:T(8,128)S(1)}, f32[16,8,...) fusion(f32[16,8,256]{2,1,0:T(8,128)S(1)} %copy-done.63, ...), kind=kLoop, calls=%fused_computation.597 | loop fusion | flops 8093696 | bytes 21266432 | tf_op jit(solution)/shard_map/sub | solution.py:137
  29.0 0.1 add_bitcast_fusion.3
  29.1 0.3 copy-done.1
  30.5 2.9 %add_bitcast_fusion.2 = (f32[1,16,8,256]{3,2,1,0:T(8,128)S(1)}, f32[16,8,256]{2,1,0:T(8,128)}, f32[16,8,256]{2,1,0:T(8,128)}, f32[16,8,256]{2,1,0:T(8,128)}, f32...) fusion(pred[1,1,16,8,256]{4,3,2,1,0:T(8,128)(4,1)S(1)} %get-tup, ...), kind=kLoop, calls=%fused_computation.248 | loop fusion | flops 2654208 | bytes 8454144 | tf_op jit(solution)/shard_map/stack | solution.py:114
  33.4 0.6 copy-done.69
  34.1 0.8 fusion.4
  35.1 0.3 convolution_bitcast_fusion.2
  35.4 0.2 copy-done.113
  35.7 0.2 fusion
  35.9 4.3 %psum.28 = bf16[1,3,7,7,128]{4,2,3,1,0:T(8,128)(2,1)S(1)} all-reduce(bf16[1,3,7,7,128]{4,2,3,1,0:T(8,128)(2,1)S(1)} %fusion), channel_id=1, replica_groups=mesh['group'=2,'slab'=4,'subj'=2,'yslab'=2] {'yslab'}, use_global_device_ids=true, to_apply=%region_0.1 | all-reduce | flops 18816 | bytes 75264 | tf_op jit(solution)/shard_map/psum | solution.py:142
  40.2 0.6 copy-done.45
  40.9 3.8 %collective-permute-start.4 = (f32[1,3,3,7,128]{4,2,3,1,0:T(4,128)S(1)}, f32[1,3,3,7,128]{4,2,3,1,0:T(4,128)S(1)}, u32[]{:S(2)}, u32[]{:S(2)}) collective-permute-start(f32[1,3,3,7,128]{4,2,3,1,0:T(4,128)S(1)} %slice.1053), channel_id=1, source_target_pairs={{0,4},{4,8},{8,12},{1,5},{5,9},{9,13},{2,6},{6,10},{10,14},{3,7},{... | collective-permute-start | bytes 96776 | tf_op jit(solution)/shard_map/ppermute | solution.py:30
  44.6 13.4 %all-gather = f32[4,3,3,7,128]{4,3,2,1,0:T(8,128)S(1)} all-gather(f32[1,3,3,7,128]{4,3,2,1,0:T(8,128)S(1)} %copy.21), channel_id=2, replica_groups=mesh['group'=2,'slab'=4,'subj'=2,'yslab'=2] {'slab'}, dimensions={0}, use_global_device_ids=true | all-gather | bytes 161280 | tf_op jit(solution)/shard_map/all_gather | solution.py:35
  58.1 0.7 slice-done
  58.8 0.1 scatter-add.6
  59.0 13.4 %all_gather.18 = bf16[1,3,16,7,128]{4,3,1,0,2:T(8,128)(2,1)S(1)} all-gather(bf16[1,3,4,7,128]{4,3,1,0,2:T(8,128)(2,1)S(1)} %copy.20), channel_id=1, replica_groups=mesh['group'=2,'slab'=4,'subj'=2,'yslab'=2] {'slab'}, dimensions={2}, use_global_device_ids=true | all-gather | bytes 107520 | tf_op jit(solution)/shard_map/all_gather | solution.py:147
  72.5 0.7 fusion.172
  74.1 1.1 copy_subtract_fusion
  75.3 1.1 convolution_bitcast_fusion.4
  76.4 0.4 convolution_bitcast_fusion.1
  76.9 1.5 %multiply_add_fusion = (f32[3,16,8,256]{3,2,1,0:T(8,128)S(1)}, f32[3,16,8,256]{3,2,1,0:T(8,128)}) fusion(f32[3,16,8,128]{3,2,1,0:T(8,128)S(1)} %convolution_bitcast_fusion.1, f32[256]{0:T(256)S(1)} %get-tuple-element.193, s32[256]{0:T(256)S(1)} %copy-done.78, f32[256]{0:T(256)S(1)} %get-tuple-element.192, s32[256]{0:T(256)S(1)} %copy-done.82, ...), kind=kOutput, calls=%fused_computation.31 | convolution fusion | flops 151552000 | bytes 991232 | tf_op jit(solution)/shard_map/czyg,xg->czyx/dot_general | solution.py:63
  78.6 3.0 %subtract_bitcast_fusion = (f32[1,16,8,256]{3,2,1,0:T(8,128)}, f32[16,8,256]{2,1,0:T(8,128)S(1)}, f32[16,8,256]{2,1,0:T(8,128)S(1)}, f32[16,8,256]{2,1,0:T(8,128...) fusion(pred[1,1,16,8,256]{4,3,2,1,0:T(8,128)(4,1)S(1)} %get-tup, ...), kind=kLoop, calls=%fused_computation.191 | loop fusion | flops 4227072 | bytes 8716288 | tf_op jit(solution)/shard_map/stack | solution.py:114
  81.7 0.8 add_bitcast_fusion.1
  82.6 0.1 copy-done.52
  82.9 0.5 copy-done.47
  83.5 0.2 add_bitcast_fusion
  83.7 21.6 %all-reduce.4.cloned.1.call-done = (f32[16,8,256]{2,1,0:T(8,128)}, f32[16,8,256]{2,1,0:T(8,128)}) async-done(((f32[16,8,256]{2,1,0:T(8,128)}, f32[16,8,256]{2,1,0:T(8,128)}), (f32[16,8,256]{2,1,0:T(8,128)}, f32[16,8,256]{2,1,0:T(8,128)})) %all-reduce.4.cloned.1.call-update) | async-done | bytes 262160 | tf_op jit(solution)/shard_map/psum | solution.py:141
  105.3 0.9 multiply_subtract_fusion
  106.3 0.6 copy-done.67
  107.0 0.8 fusion.11
  107.9 0.3 convolution_bitcast_fusion
  108.2 0.2 copy-done.115
  108.6 0.2 fusion.1
  108.8 3.5 %psum.31 = bf16[1,3,7,7,128]{4,2,3,1,0:T(8,128)(2,1)S(1)} all-reduce(bf16[1,3,7,7,128]{4,2,3,1,0:T(8,128)(2,1)S(1)} %fusion.1), channel_id=1, replica_groups=mesh['group'=2,'slab'=4,'subj'=2,'yslab'=2] {'yslab'}, use_global_device_ids=true, to_apply=%region_6.7 | all-reduce | flops 18816 | bytes 75264 | tf_op jit(solution)/shard_map/psum | solution.py:142
  112.4 0.6 copy-done.46
  113.0 0.3 copy-done.62
  113.3 0.7 broadcast_multiply_fusion
  114.0 3.4 %collective-permute-start.5 = (f32[1,3,3,7,128]{4,2,3,1,0:T(4,128)S(1)}, f32[1,3,3,7,128]{4,2,3,1,0:T(4,128)S(1)}, u32[]{:S(2)}, u32[]{:S(2)}) collective-permute-start(f32[1,3,3,7,128]{4,2,3,1,0:T(4,128)S(1)} %slice.1059), channel_id=1, source_target_pairs={{0,4},{4,8},{8,12},{1,5},{5,9},{9,13},{2,6},{6,10},{10,14},{3,7},{... | collective-permute-start | bytes 96776 | tf_op jit(solution)/shard_map/ppermute | solution.py:30
  117.4 13.4 %all-gather.1 = f32[4,3,3,7,128]{4,3,2,1,0:T(8,128)S(1)} all-gather(f32[1,3,3,7,128]{4,3,2,1,0:T(8,128)S(1)} %copy.30), channel_id=3, replica_groups=mesh['group'=2,'slab'=4,'subj'=2,'yslab'=2] {'slab'}, dimensions={0}, use_global_device_ids=true | all-gather | bytes 161280 | tf_op jit(solution)/shard_map/all_gather | solution.py:35
  130.9 0.7 slice-done.1
  131.6 0.1 scatter-add.9
  131.7 13.3 %all_gather.21 = bf16[1,3,16,7,128]{4,3,1,0,2:T(8,128)(2,1)S(1)} all-gather(bf16[1,3,4,7,128]{4,3,1,0,2:T(8,128)(2,1)S(1)} %copy.29), channel_id=1, replica_groups=mesh['group'=2,'slab'=4,'subj'=2,'yslab'=2] {'slab'}, dimensions={2}, use_global_device_ids=true | all-gather | bytes 107520 | tf_op jit(solution)/shard_map/all_gather | solution.py:147
  145.1 0.6 fusion.171
  146.4 0.9 copy.33
  (320 shorter events, 2.9 us)
Async XLA Ops:
  7.2 98.1 %all-reduce.4.cloned.1.call-start = ((), (), s32[]{:S(2)}) async-start(), calls=%async_computation | async-start | bytes 524288 | tf_op jit(solution)/shard_map/psum | solution.py:141
  7.9 9.6 %collective-permute-start.1 = (bf16[1,2,8,256]{3,2,1,0:T(8,128)(2,1)S(1)}, bf16[1,2,8,256]{3,2,1,0:T(8,128)(2,1)S(1)}, u32[]{:S(2)}, u32[]{:S(2)}) collective-permute-start(bf16[1,2,8,256]{3,2,1,0:T(8,128)(2,1)S(1)} %get-tuple-element.163), channel_id=1, source_target_pairs={{4,0},{8,4},{12,8},{5,1},{9,5},{13,9},{6,2},{10,6},{14,10},{7,3},{... | collective-permute-start | bytes 24584 | tf_op jit(solution)/shard_map/ppermute | solution.py:22
  9.2 7.9 %collective-permute-start = (bf16[1,2,8,256]{3,2,1,0:T(8,128)(2,1)S(1)}, bf16[1,2,8,256]{3,2,1,0:T(8,128)(2,1)S(1)}, u32[]{:S(2)}, u32[]{:S(2)}) collective-permute-start(bf16[1,2,8,256]{3,2,1,0:T(8,128)(2,1)S(1)} %get-tuple-element.164), channel_id=1, source_target_pairs={{0,4},{4,8},{8,12},{1,5},{5,9},{9,13},{2,6},{6,10},{10,14},{3,7},{... | collective-permute-start | bytes 24584 | tf_op jit(solution)/shard_map/ppermute | solution.py:21
  14.8 1.7 %copy-start.84 = (f32[8]{0:T(128)}, f32[8]{0:T(128)S(1)}, u32[]{:S(2)}) copy-start(f32[8]{0:T(128)S(1)} %get-tuple-element.180) | copy-start | bytes 100
  14.8 1.7 %copy-start.87 = (f32[8]{0:T(128)}, f32[8]{0:T(128)S(1)}, u32[]{:S(2)}) copy-start(f32[8]{0:T(128)S(1)} %get-tuple-element.181) | copy-start | bytes 100
  14.9 1.7 %copy-start.90 = (s32[8]{0:T(128)}, s32[8]{0:T(128)S(1)}, u32[]{:S(2)}) copy-start(s32[8]{0:T(128)S(1)} %get-tuple-element.184) | copy-start | bytes 100
  14.9 1.7 %copy-start.93 = (s32[8]{0:T(128)}, s32[8]{0:T(128)S(1)}, u32[]{:S(2)}) copy-start(s32[8]{0:T(128)S(1)} %get-tuple-element.185) | copy-start | bytes 100
  14.9 1.7 %copy-start.96 = (s32[8]{0:T(128)}, s32[8]{0:T(128)S(1)}, u32[]{:S(2)}) copy-start(s32[8]{0:T(128)S(1)} %get-tuple-element.172) | copy-start | bytes 100
  14.9 1.7 %copy-start.100 = (s32[8]{0:T(128)}, s32[8]{0:T(128)S(1)}, u32[]{:S(2)}) copy-start(s32[8]{0:T(128)S(1)} %get-tuple-element.173) | copy-start | bytes 100
  15.0 1.7 %copy-start.108 = (f32[8]{0:T(128)}, f32[8]{0:T(128)S(1)}, u32[]{:S(2)}) copy-start(f32[8]{0:T(128)S(1)} %get-tuple-element.175) | copy-start | bytes 100
  15.1 18.3 %copy-start.65 = (f32[256]{0:T(256)}, f32[256]{0:T(256)S(1)}, u32[]{:S(2)}) copy-start(f32[256]{0:T(256)S(1)} %get-tuple-element.191) | copy-start | bytes 3076
  15.2 5.2 %copy-start.68 = (s32[256]{0:T(256)}, s32[256]{0:T(256)S(1)}, u32[]{:S(2)}) copy-start(s32[256]{0:T(256)S(1)} %get-tuple-element.188) | copy-start | bytes 3076
  15.2 5.2 %copy-start.72 = (s32[256]{0:T(256)}, s32[256]{0:T(256)S(1)}, u32[]{:S(2)}) copy-start(s32[256]{0:T(256)S(1)} %get-tuple-element.189) | copy-start | bytes 3076
  17.1 3.3 %copy-start.76 = (s32[256]{0:T(256)}, s32[256]{0:T(256)S(1)}, u32[]{:S(2)}) copy-start(s32[256]{0:T(256)S(1)} %get-tuple-element.186) | copy-start | bytes 3076
  17.1 3.3 %copy-start.80 = (s32[256]{0:T(256)}, s32[256]{0:T(256)S(1)}, u32[]{:S(2)}) copy-start(s32[256]{0:T(256)S(1)} %get-tuple-element.187) | copy-start | bytes 3076
  17.6 4.4 %collective-permute-start.2 = (bf16[1,20,2,256]{3,2,1,0:T(2,128)(2,1)S(1)}, bf16[1,20,2,256]{3,2,1,0:T(2,128)(2,1)S(1)}, u32[]{:S(2)}, u32[]{:S(2)}) collective-permute-start(bf16[1,20,2,256]{3,2,1,0:T(2,128)(2,1)S(1)} %get-tuple-element.161), channel_id=1, source_target_pairs={{0,1},{2,3},{4,5},{6,7},{8,9},{10,11},{12,13},{14,15},{16,17},{18,... | collective-permute-start | bytes 61448 | tf_op jit(solution)/shard_map/ppermute | solution.py:21
  19.0 3.1 %collective-permute-start.3 = (bf16[1,20,2,256]{3,2,1,0:T(2,128)(2,1)S(1)}, bf16[1,20,2,256]{3,2,1,0:T(2,128)(2,1)S(1)}, u32[]{:S(2)}, u32[]{:S(2)}) collective-permute-start(bf16[1,20,2,256]{3,2,1,0:T(2,128)(2,1)S(1)} %get-tuple-element.162), channel_id=1, source_target_pairs={{1,0},{3,2},{5,4},{7,6},{9,8},{11,10},{13,12},{15,14},{17,16},{19,... | collective-permute-start | bytes 61448 | tf_op jit(solution)/shard_map/ppermute | solution.py:22
  30.5 2.9 %copy-start.57 = (f32[3,16,8,256]{3,2,1,0:T(8,128)S(1)}, f32[3,16,8,256]{3,2,1,0:T(8,128)}, u32[]{:S(2)}) copy-start(f32[3,16,8,256]{3,2,1,0:T(8,128)} %get-tuple-element.166) | copy-start | bytes 1179652
  30.5 3.0 %copy-start.73 = (s32[256]{0:T(256)S(1)}, s32[256]{0:T(256)}, u32[]{:S(2)}) copy-start(s32[256]{0:T(256)} %copy-done.72) | copy-start | bytes 3076
  30.5 3.0 %copy-start.77 = (s32[256]{0:T(256)S(1)}, s32[256]{0:T(256)}, u32[]{:S(2)}) copy-start(s32[256]{0:T(256)} %copy-done.76) | copy-start | bytes 3076
  30.5 3.0 %copy-start.81 = (s32[256]{0:T(256)S(1)}, s32[256]{0:T(256)}, u32[]{:S(2)}) copy-start(s32[256]{0:T(256)} %copy-done.80) | copy-start | bytes 3076
  40.9 17.2 %collective-permute-start.4 = (f32[1,3,3,7,128]{4,2,3,1,0:T(4,128)S(1)}, f32[1,3,3,7,128]{4,2,3,1,0:T(4,128)S(1)}, u32[]{:S(2)}, u32[]{:S(2)}) collective-permute-start(f32[1,3,3,7,128]{4,2,3,1,0:T(4,128)S(1)} %slice.1053), channel_id=1, source_target_pairs={{0,4},{4,8},{8,12},{1,5},{5,9},{9,13},{2,6},{6,10},{10,14},{3,7},{... | collective-permute-start | bytes 96776 | tf_op jit(solution)/shard_map/ppermute | solution.py:30
  72.4 2.8 %copy-start.114 = (s32[16]{0:T(128)S(1)}, s32[16]{0:T(128)}, u32[]{:S(2)}) copy-start(s32[16]{0:T(128)} %copy-done.112) | copy-start | bytes 196
  72.4 2.8 %copy-start.118 = (s32[16]{0:T(128)S(1)}, s32[16]{0:T(128)}, u32[]{:S(2)}) copy-start(s32[16]{0:T(128)} %copy-done.116) | copy-start | bytes 196
  72.4 2.8 %copy-start.122 = (f32[16]{0:T(128)S(1)}, f32[16]{0:T(128)}, u32[]{:S(2)}) copy-start(f32[16]{0:T(128)} %copy-done.120) | copy-start | bytes 196
  72.4 2.8 %copy-start.126 = (f32[16]{0:T(128)S(1)}, f32[16]{0:T(128)}, u32[]{:S(2)}) copy-start(f32[16]{0:T(128)} %copy-done.124) | copy-start | bytes 196
  72.4 2.8 %copy-start.130 = (f32[16]{0:T(128)S(1)}, f32[16]{0:T(128)}, u32[]{:S(2)}) copy-start(f32[16]{0:T(128)} %copy-done.128) | copy-start | bytes 196
  72.4 2.8 %copy-start.134 = (f32[16]{0:T(128)S(1)}, f32[16]{0:T(128)}, u32[]{:S(2)}) copy-start(f32[16]{0:T(128)} %copy-done.132) | copy-start | bytes 196
  72.4 2.8 %copy-start.138 = (s32[16]{0:T(128)S(1)}, s32[16]{0:T(128)}, u32[]{:S(2)}) copy-start(s32[16]{0:T(128)} %copy-done.136) | copy-start | bytes 196
  72.4 3.9 %copy-start.106 = (f32[8]{0:T(128)S(1)}, f32[8]{0:T(128)}, u32[]{:S(2)}) copy-start(f32[8]{0:T(128)} %copy-done.104) | copy-start | bytes 100
  72.5 3.9 %copy-start.110 = (f32[8]{0:T(128)S(1)}, f32[8]{0:T(128)}, u32[]{:S(2)}) copy-start(f32[8]{0:T(128)} %copy-done.108) | copy-start | bytes 100
  73.9 2.4 %copy-start.98 = (s32[8]{0:T(128)S(1)}, s32[8]{0:T(128)}, u32[]{:S(2)}) copy-start(s32[8]{0:T(128)} %copy-done.96) | copy-start | bytes 100
  73.9 2.4 %copy-start.102 = (s32[8]{0:T(128)S(1)}, s32[8]{0:T(128)}, u32[]{:S(2)}) copy-start(s32[8]{0:T(128)} %copy-done.100) | copy-start | bytes 100
  74.0 2.9 %copy-start.70 = (s32[256]{0:T(256)S(1)}, s32[256]{0:T(256)}, u32[]{:S(2)}) copy-start(s32[256]{0:T(256)} %copy-done.68) | copy-start | bytes 3076
  74.0 2.9 %copy-start.74 = (s32[256]{0:T(256)S(1)}, s32[256]{0:T(256)}, u32[]{:S(2)}) copy-start(s32[256]{0:T(256)} %copy-done.72) | copy-start | bytes 3076
  74.0 2.9 %copy-start.78 = (s32[256]{0:T(256)S(1)}, s32[256]{0:T(256)}, u32[]{:S(2)}) copy-start(s32[256]{0:T(256)} %copy-done.76) | copy-start | bytes 3076
  74.0 2.9 %copy-start.82 = (s32[256]{0:T(256)S(1)}, s32[256]{0:T(256)}, u32[]{:S(2)}) copy-start(s32[256]{0:T(256)} %copy-done.80) | copy-start | bytes 3076
  74.0 4.5 %copy-start.28 = (f32[16,8,256]{2,1,0:T(8,128)S(1)}, f32[16,8,256]{2,1,0:T(8,128)}, u32[]{:S(2)}) copy-start(f32[16,8,256]{2,1,0:T(8,128)} %copy-done.27) | copy-start | bytes 393220
  74.0 4.5 %copy-start.30 = (f32[16,8,256]{2,1,0:T(8,128)S(1)}, f32[16,8,256]{2,1,0:T(8,128)}, u32[]{:S(2)}) copy-start(f32[16,8,256]{2,1,0:T(8,128)} %copy-done.29) | copy-start | bytes 393220
  74.0 4.5 %copy-start.32 = (f32[16,8,256]{2,1,0:T(8,128)S(1)}, f32[16,8,256]{2,1,0:T(8,128)}, u32[]{:S(2)}) copy-start(f32[16,8,256]{2,1,0:T(8,128)} %copy-done.31) | copy-start | bytes 393220
  74.0 4.5 %copy-start.34 = (f32[16,8,256]{2,1,0:T(8,128)S(1)}, f32[16,8,256]{2,1,0:T(8,128)}, u32[]{:S(2)}) copy-start(f32[16,8,256]{2,1,0:T(8,128)} %copy-done.33) | copy-start | bytes 393220
  74.0 4.5 %copy-start.36 = (f32[16,8,256]{2,1,0:T(8,128)S(1)}, f32[16,8,256]{2,1,0:T(8,128)}, u32[]{:S(2)}) copy-start(f32[16,8,256]{2,1,0:T(8,128)} %copy-done.35) | copy-start | bytes 393220
  74.0 4.5 %copy-start.38 = (f32[16,8,256]{2,1,0:T(8,128)S(1)}, f32[16,8,256]{2,1,0:T(8,128)}, u32[]{:S(2)}) copy-start(f32[16,8,256]{2,1,0:T(8,128)} %copy-done.37) | copy-start | bytes 393220
  75.1 3.4 %copy-start.26 = (f32[16,8,256]{2,1,0:T(8,128)S(1)}, f32[16,8,256]{2,1,0:T(8,128)}, u32[]{:S(2)}) copy-start(f32[16,8,256]{2,1,0:T(8,128)} %copy-done.25) | copy-start | bytes 393220
  75.2 3.3 %copy-start.22 = (f32[16,8,256]{2,1,0:T(8,128)S(1)}, f32[16,8,256]{2,1,0:T(8,128)}, u32[]{:S(2)}) copy-start(f32[16,8,256]{2,1,0:T(8,128)} %copy-done.21) | copy-start | bytes 393220
  75.2 3.3 %copy-start.24 = (f32[16,8,256]{2,1,0:T(8,128)S(1)}, f32[16,8,256]{2,1,0:T(8,128)}, u32[]{:S(2)}) copy-start(f32[16,8,256]{2,1,0:T(8,128)} %copy-done.23) | copy-start | bytes 393220
  76.4 2.1 %copy-start.16 = (f32[16,8,256]{2,1,0:T(8,128)S(1)}, f32[16,8,256]{2,1,0:T(8,128)}, u32[]{:S(2)}) copy-start(f32[16,8,256]{2,1,0:T(8,128)} %copy-done.15) | copy-start | bytes 393220
  76.4 2.1 %copy-start.18 = (f32[16,8,256]{2,1,0:T(8,128)S(1)}, f32[16,8,256]{2,1,0:T(8,128)}, u32[]{:S(2)}) copy-start(f32[16,8,256]{2,1,0:T(8,128)} %copy-done.17) | copy-start | bytes 393220
  76.4 2.1 %copy-start.20 = (f32[16,8,256]{2,1,0:T(8,128)S(1)}, f32[16,8,256]{2,1,0:T(8,128)}, u32[]{:S(2)}) copy-start(f32[16,8,256]{2,1,0:T(8,128)} %copy-done.19) | copy-start | bytes 393220
  76.9 1.7 %copy-start.2 = (f32[16,8,256]{2,1,0:T(8,128)S(1)}, f32[16,8,256]{2,1,0:T(8,128)}, u32[]{:S(2)}) copy-start(f32[16,8,256]{2,1,0:T(8,128)} %copy-done.1) | copy-start | bytes 393220
  76.9 1.7 %copy-start.4 = (f32[16,8,256]{2,1,0:T(8,128)S(1)}, f32[16,8,256]{2,1,0:T(8,128)}, u32[]{:S(2)}) copy-start(f32[16,8,256]{2,1,0:T(8,128)} %copy-done.3) | copy-start | bytes 393220
  76.9 1.7 %copy-start.6 = (f32[16,8,256]{2,1,0:T(8,128)S(1)}, f32[16,8,256]{2,1,0:T(8,128)}, u32[]{:S(2)}) copy-start(f32[16,8,256]{2,1,0:T(8,128)} %copy-done.5) | copy-start | bytes 393220
  76.9 1.7 %copy-start.8 = (f32[16,8,256]{2,1,0:T(8,128)S(1)}, f32[16,8,256]{2,1,0:T(8,128)}, u32[]{:S(2)}) copy-start(f32[16,8,256]{2,1,0:T(8,128)} %copy-done.7) | copy-start | bytes 393220
  76.9 1.7 %copy-start.10 = (f32[16,8,256]{2,1,0:T(8,128)S(1)}, f32[16,8,256]{2,1,0:T(8,128)}, u32[]{:S(2)}) copy-start(f32[16,8,256]{2,1,0:T(8,128)} %copy-done.9) | copy-start | bytes 393220
  76.9 1.7 %copy-start.12 = (f32[16,8,256]{2,1,0:T(8,128)S(1)}, f32[16,8,256]{2,1,0:T(8,128)}, u32[]{:S(2)}) copy-start(f32[16,8,256]{2,1,0:T(8,128)} %copy-done.11) | copy-start | bytes 393220
  76.9 1.7 %copy-start.14 = (f32[16,8,256]{2,1,0:T(8,128)S(1)}, f32[16,8,256]{2,1,0:T(8,128)}, u32[]{:S(2)}) copy-start(f32[16,8,256]{2,1,0:T(8,128)} %copy-done.13) | copy-start | bytes 393220
  83.5 21.8 %copy-start = (f32[16,8,256]{2,1,0:T(8,128)S(1)}, f32[16,8,256]{2,1,0:T(8,128)}, u32[]{:S(2)}) copy-start(f32[16,8,256]{2,1,0:T(8,128)} %get-tuple-element.118) | copy-start | bytes 393220
  83.5 22.7 %copy-start.61 = (f32[1,16,8,256]{3,2,1,0:T(8,128)S(1)}, f32[1,16,8,256]{3,2,1,0:T(8,128)}, u32[]{:S(2)}) copy-start(f32[1,16,8,256]{3,2,1,0:T(8,128)} %get-tuple-element.34) | copy-start | bytes 393220
  83.5 22.7 %copy-start.71 = (s32[256]{0:T(256)S(1)}, s32[256]{0:T(256)}, u32[]{:S(2)}) copy-start(s32[256]{0:T(256)} %copy-done.68) | copy-start | bytes 3076
  83.5 22.8 %copy-start.75 = (s32[256]{0:T(256)S(1)}, s32[256]{0:T(256)}, u32[]{:S(2)}) copy-start(s32[256]{0:T(256)} %copy-done.72) | copy-start | bytes 3076
  83.5 22.8 %copy-start.79 = (s32[256]{0:T(256)S(1)}, s32[256]{0:T(256)}, u32[]{:S(2)}) copy-start(s32[256]{0:T(256)} %copy-done.76) | copy-start | bytes 3076
  83.5 22.8 %copy-start.83 = (s32[256]{0:T(256)S(1)}, s32[256]{0:T(256)}, u32[]{:S(2)}) copy-start(s32[256]{0:T(256)} %copy-done.80) | copy-start | bytes 3076
  83.7 22.6 %copy-start.58 = (f32[3,16,8,256]{3,2,1,0:T(8,128)S(1)}, f32[3,16,8,256]{3,2,1,0:T(8,128)}, u32[]{:S(2)}) copy-start(f32[3,16,8,256]{3,2,1,0:T(8,128)} %get-tuple-element.169) | copy-start | bytes 1179652
  114.0 16.9 %collective-permute-start.5 = (f32[1,3,3,7,128]{4,2,3,1,0:T(4,128)S(1)}, f32[1,3,3,7,128]{4,2,3,1,0:T(4,128)S(1)}, u32[]{:S(2)}, u32[]{:S(2)}) collective-permute-start(f32[1,3,3,7,128]{4,2,3,1,0:T(4,128)S(1)} %slice.1059), channel_id=1, source_target_pairs={{0,4},{4,8},{8,12},{1,5},{5,9},{9,13},{2,6},{6,10},{10,14},{3,7},{... | collective-permute-start | bytes 96776 | tf_op jit(solution)/shard_map/ppermute | solution.py:30
  (88 other events, 83.4 us)
Sparse Core Ops, SparseCore 0:
  82.6 22.6 all-reduce.3
